TPU v7x, 32 devices: a whole 2x2x4 slice. The times are simulated.
32 devices in a mesh: tile: 4 (over y, x), mom: 2 (over core), ewin: 4 (over z).
Axes of the slice: x: 2, y: 2, z: 4, core: 2. Of those that a mesh axis runs over, the one named last changes fastest.
Arguments:
- green_ret: bfloat16 [2, 4, 4, 512, 1024], P('mom', 'ewin', 'tile'), may hold values from -0.25 to 0.25
- injection: float32 [2, 4, 4, 512], P('mom', 'ewin', 'tile'), may hold values from 0.1 to 1
- mom_shift: int32 [4], replicated, may hold values from 0 to 7, as said below
- phon_off: int32 [8], replicated, may hold values from -4 to 4
- coupling: float32 [4, 8], replicated, may hold values from 0.05 to 1
- tile_nbr: int32 [4, 4], replicated, may hold values from 0 to 3
Outputs:
- sigma_less: bfloat16 [2, 4, 4, 512, 1024], P('mom', 'ewin', None, 'tile')
Inputs may be any that keep to these rules, and one draw needn't show every extreme that they name: `mom_shift`: every residue from 0 to 1 appears among the 4 shifts taken modulo 2.
All inputs are finite; a program needn't handle non-finite values.
Results may differ from a plain program's by a relative error of at most 0.0036.
Values may be sent and summed in bfloat16 or wider, within the bound.
A program may use at most 64 MiB of HBM per device.

v0:
```python
import jax
import jax.numpy as jnp
from jax import lax
from jax.sharding import PartitionSpec as P

HW = 4
NW = 8


def with_halo(shard, sides, width):
    for axis, dim in sides:
        peers, length = (lax.axis_size(axis), shard.shape[dim])
        up = [(i, (i + 1) % peers) for i in range(peers - 1)]
        down = [(j, i) for i, j in up]
        last = lax.slice_in_dim(shard, length - width, length, axis=dim)
        initial = lax.slice_in_dim(shard, 0, width, axis=dim)
        before = lax.ppermute(last, axis, up)
        after = lax.ppermute(initial, axis, down)
        shard = jnp.concatenate([before, shard, after], axis=dim)
    return shard


def on_device(green_ret, injection, mom_shift, phon_off, coupling, tile_nbr):
    blocks = green_ret[0, 0]
    gamma = injection[0, 0]
    orbitals = blocks.shape[1]
    ntiles = lax.axis_size("tile")
    per_tile = orbitals // ntiles
    real_part = blocks[:, :, :orbitals].astype(jnp.float32)
    imag_part = blocks[:, :, orbitals:].astype(jnp.float32)
    scale = gamma[:, None, :]
    left_re = jnp.concatenate([real_part * scale, imag_part * scale], axis=2).astype(jnp.bfloat16)
    left_im = jnp.concatenate([imag_part * scale, -real_part * scale], axis=2).astype(jnp.bfloat16)
    real_out = jnp.einsum("prk,pck->prc", left_re, blocks, preferred_element_type=jnp.float32)
    imag_out = jnp.einsum("prk,pck->prc", left_im, blocks, preferred_element_type=jnp.float32)
    payload = jnp.concatenate([real_out, imag_out], axis=2).astype(jnp.bfloat16)
    exchanged = lax.all_to_all(payload, "tile", split_axis=1, concat_axis=0, tiled=True)
    energies = exchanged.shape[0]
    rimmed = with_halo(exchanged, (("ewin", 0),), HW)
    extended = lax.all_gather(rimmed[None], "mom", axis=0, tiled=True)
    nmom = lax.axis_size("mom")
    here = lax.axis_index("mom")
    source = jnp.mod(here - mom_shift, nmom)
    onehot = (source[:, None] == jnp.arange(nmom, dtype=jnp.int32)[None, :]).astype(jnp.float32)
    weights = jnp.dot(onehot.T, coupling, precision=lax.Precision.HIGHEST)
    total = jnp.zeros(exchanged.shape, jnp.float32)
    for offset in range(NW):
        start = HW + phon_off[offset]
        piece = lax.dynamic_slice_in_dim(extended, start, energies, 1)
        for moment in range(nmom):
            total = total + weights[moment, offset] * piece[moment].astype(jnp.float32)
    tile_here = lax.axis_index("tile")
    neighbours = lax.dynamic_index_in_dim(tile_nbr, tile_here, 0, keepdims=False)
    coltile = jnp.arange(orbitals, dtype=jnp.int32) // per_tile
    colmask = jnp.any(coltile[:, None] == neighbours[None, :], axis=1).astype(jnp.float32)
    colmask = jnp.concatenate([colmask, colmask])
    result = (total * colmask[None, None, :]).astype(jnp.bfloat16)
    return result[None, None]


def solution(mesh):
    placed = (
        P("mom", "ewin", "tile", None, None),
        P("mom", "ewin", "tile", None),
        P(),
        P(),
        P(),
        P(),
    )
    return jax.shard_map(
        on_device,
        mesh=mesh,
        in_specs=placed,
        out_specs=P("mom", "ewin", None, "tile", None),
        check_vma=False,
    )
```

profile of v0, /device:TPU:0, one launch (start us, length us, event | category | flops | bytes accessed | tf_op | source)
XLA Modules:
  0.0 113.0 jit_solution(7186449994337882947)
XLA Ops:
  6.5 1.6 %fusion.17 = (bf16[512,512]{1,0:T(8,128)(2,1)S(1)}, bf16[512,512]{1,0:T(8,128)(2,1)S(1)}, bf16[512,512]{1,0:T(8,128)(2,1)S(1)}) fusion(f32[512]{0:T(512)} %bitcast.71, bf16[1,512,1024]{2,1,0:T(8,128)(2,1)} %bitcast.70), kind=kLoop, calls=%fused_computation.25 | loop fusion | flops 2359296 | bytes 2623488 | tf_op jit(solution)/shard_map/concatenate | solution.py:32
  8.2 0.7 fusion.2
  8.9 0.7 fusion.3
  9.7 0.1 pad_maximum_fusion.1
  9.8 2.0 %copy.10 = bf16[1,512,1024]{2,0,1:T(2,128)(2,1)S(1)} copy(bf16[1,512,1024]{1,2,0:T(8,128)(2,1)S(1)} %pad_maximum_fusion.1) | data formatting | bytes 2097152 | tf_op jit(solution)/shard_map/concatenate | solution.py:36
  11.7 0.5 broadcast.191
  12.3 7.3 %reduce = bf16[512,1024]{1,0:T(8,128)(2,1)S(1)} reduce(bf16[512,1,1024]{2,1,0:T(2,128)(2,1)S(1)} %bitcast.66, bf16[]{:T(256)} %broadcast.191), dimensions={1}, to_apply=%bitcast.61.reduce_sub_computation | reduce | bytes 2097154
  19.6 0.8 reshape.449
  20.4 19.1 %all_to_all.12 = bf16[4,2,65536]{2,1,0:T(2,128)(2,1)S(1)} all-to-all(bf16[4,2,65536]{2,1,0:T(2,128)(2,1)S(1)} %reshape.449), channel_id=1, replica_groups=mesh['tile'=4,'mom'=2,'ewin'=4] {'tile'}, dimensions={0} | all-to-all | bytes 2097152 | tf_op jit(solution)/shard_map/all_to_all | solution.py:37
  39.5 0.9 reshape.450
  40.5 0.4 copy.11
  40.9 3.5 %collective-permute-start = (bf16[4,128,1024]{2,1,0:T(8,128)(2,1)S(1)}, bf16[4,128,1024]{2,1,0:T(8,128)(2,1)S(1)}, u32[]{:S(2)}, u32[]{:S(2)}) collective-permute-start(bf16[4,128,1024]{2,1,0:T(8,128)(2,1)S(1)} %bitcast.67), channel_id=1, source_target_pairs={{0,1},{1,2},{2,3},{4,5},{5,6},{6,7},{8,9},{9,10},{10,11},{12,13},{... | collective-permute-start | bytes 3145736 | tf_op jit(solution)/shard_map/ppermute | solution.py:17
  44.4 1.5 %collective-permute-start.1 = (bf16[4,128,1024]{2,1,0:T(8,128)(2,1)S(1)}, bf16[4,128,1024]{2,1,0:T(8,128)(2,1)S(1)}, u32[]{:S(2)}, u32[]{:S(2)}) collective-permute-start(bf16[4,128,1024]{2,1,0:T(8,128)(2,1)S(1)} %bitcast.68), channel_id=1, source_target_pairs={{1,0},{2,1},{3,2},{5,4},{6,5},{7,6},{9,8},{10,9},{11,10},{13,12},{... | collective-permute-start | bytes 3145736 | tf_op jit(solution)/shard_map/ppermute | solution.py:18
  45.9 19.4 %collective-permute-done = bf16[4,128,1024]{2,1,0:T(8,128)(2,1)S(1)} collective-permute-done((bf16[4,128,1024]{2,1,0:T(8,128)(2,1)S(1)}, bf16[4,128,1024]{2,1,0:T(8,128)(2,1)S(1)}, u32[]{:S(2)}, u32[]{:S(2)}) %collective-permute-start) | collective-permute-done | bytes 1048608 | tf_op jit(solution)/shard_map/ppermute | solution.py:17
  65.2 4.2 %collective-permute-done.1 = bf16[4,128,1024]{2,1,0:T(8,128)(2,1)S(1)} collective-permute-done((bf16[4,128,1024]{2,1,0:T(8,128)(2,1)S(1)}, bf16[4,128,1024]{2,1,0:T(8,128)(2,1)S(1)}, u32[]{:S(2)}, u32[]{:S(2)}) %collective-permute-start.1) | collective-permute-done | bytes 1048608 | tf_op jit(solution)/shard_map/ppermute | solution.py:18
  69.4 1.8 %pad_maximum_fusion = bf16[12,128,1024]{2,1,0:T(8,128)(2,1)} fusion(bf16[4,128,1024]{2,1,0:T(8,128)(2,1)S(1)} %collective-permute-done.1, bf16[4,128,1024]{2,1,0:T(8,128)(2,1)S(1)} %bitcast.69, bf16[4,128,1024]{2,1,0:T(8,128)(2,1)S(1)} %collective-permute-done), kind=kLoop, calls=%fused_computation | loop fusion | flops 3145728 | bytes 6291456 | tf_op jit(solution)/shard_map/concatenate | solution.py:19
  71.3 0.6 copy-done.2
  71.9 0.7 fusion.28
  82.8 0.7 fusion.24
  83.6 0.1 compare_reduce_fusion
  83.7 0.3 fusion.21
  83.9 0.7 fusion.27
  84.6 2.6 %all-gather.3.cloned.1.call-done = bf16[24,128,1024]{2,1,0:T(8,128)(2,1)} async-done(((bf16[12,128,1024]{2,1,0:T(8,128)(2,1)}), bf16[24,128,1024]{2,1,0:T(8,128)(2,1)}) %all-gather.3.cloned.1.call-update) | async-done | bytes 6291472 | tf_op jit(solution)/shard_map/all_gather | solution.py:40
  87.2 19.0 %fusion.1 = bf16[1,1,4,128,1024]{4,3,2,1,0:T(8,128)(2,1)} fusion(bf16[2,12,128,1024]{3,2,1,0:T(8,128)(2,1)} %bitcast.64, s32[]{:T(128)S(6)} %add.344, s32[]{:T(128)S(6)} %select_n.52, s32[]{:T(128)S(6)} %select_n.51, s32[]{:T(128)S(6)} %select_n.50, s32[]{:T(128)S(6)} %select_n.49, s32[]{:T(128)S(6)} %select_n.48, s32[]{:T(128)S(6)} %select_n.47, ...), kind=kLoop, calls=%fused_computation.3 | loop fusion | flops 25690112 | bytes 17829988 | tf_op jit(solution)/shard_map/convert_element_type | solution.py:57
  (12 shorter events, 0.1 us)
Async XLA Ops:
  6.5 77.2 %copy-start = (f32[4,8]{1,0:T(4,128)S(1)}, f32[4,8]{1,0:T(4,128)}, u32[]{:S(2)}) copy-start(f32[4,8]{1,0:T(4,128)} %param.10) | copy-start | bytes 388
  6.5 1.6 %copy-start.1 = (bf16[1,1,1,512,1024]{4,3,2,1,0:T(8,128)(2,1)S(1)}, bf16[1,1,1,512,1024]{4,3,2,1,0:T(8,128)(2,1)}, u32[]{:S(2)}) copy-start(bf16[1,1,1,512,1024]{4,3,2,1,0:T(8,128)(2,1)} %param.6) | copy-start | bytes 3145732
  6.5 80.7 %all-gather.3.cloned.1.call-start = ((), (), s32[]{:S(2)}) async-start(), calls=%async_computation.1 | async-start | bytes 9437184 | tf_op jit(solution)/shard_map/all_gather | solution.py:40
  40.9 24.4 %collective-permute-start = (bf16[4,128,1024]{2,1,0:T(8,128)(2,1)S(1)}, bf16[4,128,1024]{2,1,0:T(8,128)(2,1)S(1)}, u32[]{:S(2)}, u32[]{:S(2)}) collective-permute-start(bf16[4,128,1024]{2,1,0:T(8,128)(2,1)S(1)} %bitcast.67), channel_id=1, source_target_pairs={{0,1},{1,2},{2,3},{4,5},{5,6},{6,7},{8,9},{9,10},{10,11},{12,13},{... | collective-permute-start | bytes 3145736 | tf_op jit(solution)/shard_map/ppermute | solution.py:17
  44.4 25.0 %collective-permute-start.1 = (bf16[4,128,1024]{2,1,0:T(8,128)(2,1)S(1)}, bf16[4,128,1024]{2,1,0:T(8,128)(2,1)S(1)}, u32[]{:S(2)}, u32[]{:S(2)}) collective-permute-start(bf16[4,128,1024]{2,1,0:T(8,128)(2,1)S(1)} %bitcast.68), channel_id=1, source_target_pairs={{1,0},{2,1},{3,2},{5,4},{6,5},{7,6},{9,8},{10,9},{11,10},{13,12},{... | collective-permute-start | bytes 3145736 | tf_op jit(solution)/shard_map/ppermute | solution.py:18
  71.3 0.7 copy-start.2
  71.3 12.4 %copy-start.3 = (s32[4]{0:T(128)S(1)}, s32[4]{0:T(128)}, u32[]{:S(2)}) copy-start(s32[4]{0:T(128)} %param.8) | copy-start | bytes 52
Sparse Core Ops, SparseCore 0:
  71.4 15.7 all-gather.2
where the time goes:
time: 114 us; the launch traced here: 113 us
  other arithmetic  29.9 us (26%)
  waiting for transfers between devices  26.1 us (23%)
  between operations  23.8 us (21%)
  blocking collectives  19.1 us (17%)
  local copies, waits for them, and re-layouts  7.35 us (6%)
  starting transfers between devices  5.01 us (4%)
  matrix products  1.74 us (2%)
    ppermute x1, waiting for transfers between devices, with_halo(): before = lax.ppermute(last, axis, up)  19.4 us
    all_to_all x1, blocking collectives, on_device(): lax.all_to_all(payload, 'tile', split_axis=1, concat_axis=0, tiled=True)  19.1 us
    convert_element_type x1, other arithmetic, on_device(): result = (total * colmask[None, None, :]).astype(jnp.bfloat16)  19 us
    unnamed x1, other arithmetic  7.31 us
    ppermute x1, waiting for transfers between devices, with_halo(): after = lax.ppermute(initial, axis, down)  4.18 us
    ppermute x1, starting transfers between devices, with_halo(): before = lax.ppermute(last, axis, up)  3.54 us
    unnamed x12, local copies, waits for them, and re-layouts  3.28 us
    all_gather x1, waiting for transfers between devices, on_device(): extended = lax.all_gather(rimmed[None], 'mom', axis=0, tiled=True)  2.56 us
  transfers between devices with their start and end apart: 3, of which 3 were waited for; matrix products, arithmetic and copies ran while one was open for 2% of the time, Pallas kernels for 0%

commit v1 on v0

--- a/solution.py
+++ b/solution.py
@@ -34,7 +34,10 @@
     real_out = jnp.einsum("prk,pck->prc", left_re, blocks, preferred_element_type=jnp.float32)
     imag_out = jnp.einsum("prk,pck->prc", left_im, blocks, preferred_element_type=jnp.float32)
     payload = jnp.concatenate([real_out, imag_out], axis=2).astype(jnp.bfloat16)
-    exchanged = lax.all_to_all(payload, "tile", split_axis=1, concat_axis=0, tiled=True)
+    exchanged = jnp.concatenate(
+        lax.all_to_all(jnp.stack(jnp.split(payload, lax.axis_size("tile"), axis=1)), "tile", 0, 0),
+        axis=0,
+    )
     energies = exchanged.shape[0]
     rimmed = with_halo(exchanged, (("ewin", 0),), HW)
     extended = lax.all_gather(rimmed[None], "mom", axis=0, tiled=True)

time: 114 us -> 103 us (0.904)
  other arithmetic: 29.9 us -> 21.4 us
  local copies, waits for them, and re-layouts: 7.35 us -> 5.64 us
    unnamed x1 -> x0, other arithmetic: 7.31 us -> none
    unnamed x12 -> x8, local copies, waits for them, and re-layouts: 3.28 us -> 0.64 us
    concatenate x1, other arithmetic: 1.83 us -> 0.37 us  [with_halo(): shard = jnp.concatenate([before, shard, after], axis=dim)]
where the time goes in v1:
time: 103 us
  waiting for transfers between devices  26.7 us (26%)
  between operations  23.3 us (23%)
  other arithmetic  21.4 us (21%)
  blocking collectives  19.1 us (19%)
  local copies, waits for them, and re-layouts  5.64 us (5%)
  starting transfers between devices  4.83 us (5%)
  matrix products  1.74 us (2%)
    ppermute x1, waiting for transfers between devices, with_halo(): before = lax.ppermute(last, axis, up)  19.5 us
    all_to_all x1, blocking collectives, on_device(): lax.all_to_all(jnp.stack(jnp.split(payload, lax.axis_size('tile'), axis=1...  19.1 us
    convert_element_type x1, other arithmetic, on_device(): result = (total * colmask[None, None, :]).astype(jnp.bfloat16)  19 us
    ppermute x1, waiting for transfers between devices, with_halo(): after = lax.ppermute(initial, axis, down)  4.18 us
    ppermute x1, starting transfers between devices, with_halo(): before = lax.ppermute(last, axis, up)  3.54 us
    all_gather x1, waiting for transfers between devices, on_device(): extended = lax.all_gather(rimmed[None], 'mom', axis=0, tiled=True)  3 us
    concatenate x1, local copies, waits for them, and re-layouts, with_halo(): shard = jnp.concatenate([before, shard, after], axis=dim)  2.91 us
  transfers between devices with their start and end apart: 3, of which 3 were waited for; matrix products, arithmetic and copies ran while one was open for 2% of the time, Pallas kernels for 0%

profile of v1, /device:TPU:0, one launch (start us, length us, event | category | flops | bytes accessed | tf_op | source)
XLA Modules:
  0.0 102.8 jit_solution(127673633655513251)
XLA Ops:
  6.5 0.0 copy-start
  6.5 0.0 all-gather.3.cloned.1.call-start
  6.5 1.6 %fusion.17 = (bf16[512,512]{1,0:T(8,128)(2,1)S(1)}, bf16[512,512]{1,0:T(8,128)(2,1)S(1)}, bf16[512,512]{1,0:T(8,128)(2,1)S(1)}) fusion(f32[512]{0:T(512)} %bitcast.75, bf16[1,512,1024]{2,1,0:T(8,128)(2,1)} %bitcast.74), kind=kLoop, calls=%fused_computation.31 | loop fusion | flops 2359296 | bytes 2623488 | tf_op jit(solution)/shard_map/concatenate | solution.py:32
  8.2 0.7 fusion.3
  8.9 0.7 fusion.2
  9.7 0.2 fusion.21
  9.9 0.1 pad_maximum_fusion.1
  10.0 19.1 %all_to_all.5 = bf16[4,1,128,1024]{2,3,1,0:T(8,128)(2,1)S(1)} all-to-all(bf16[4,1,128,1024]{2,3,1,0:T(8,128)(2,1)S(1)} %pad_maximum_fusion.1), channel_id=1, replica_groups=mesh['tile'=4,'mom'=2,'ewin'=4] {'tile'}, dimensions={0} | all-to-all | bytes 2097152 | tf_op jit(solution)/shard_map/all_to_all | solution.py:38
  29.1 3.5 %collective-permute-start = (bf16[4,128,1024]{1,2,0:T(8,128)(2,1)S(1)}, bf16[4,128,1024]{1,2,0:T(8,128)(2,1)S(1)}, u32[]{:S(2)}, u32[]{:S(2)}) collective-permute-start(bf16[4,128,1024]{1,2,0:T(8,128)(2,1)S(1)} %bitcast.71), channel_id=1, source_target_pairs={{0,1},{1,2},{2,3},{4,5},{5,6},{6,7},{8,9},{9,10},{10,11},{12,13},{... | collective-permute-start | bytes 3145736 | tf_op jit(solution)/shard_map/ppermute | solution.py:17
  32.7 1.3 %collective-permute-start.1 = (bf16[4,128,1024]{1,2,0:T(8,128)(2,1)S(1)}, bf16[4,128,1024]{1,2,0:T(8,128)(2,1)S(1)}, u32[]{:S(2)}, u32[]{:S(2)}) collective-permute-start(bf16[4,128,1024]{1,2,0:T(8,128)(2,1)S(1)} %bitcast.72), channel_id=1, source_target_pairs={{1,0},{2,1},{3,2},{5,4},{6,5},{7,6},{9,8},{10,9},{11,10},{13,12},{... | collective-permute-start | bytes 3145736 | tf_op jit(solution)/shard_map/ppermute | solution.py:18
  34.0 19.5 %collective-permute-done = bf16[4,128,1024]{1,2,0:T(8,128)(2,1)S(1)} collective-permute-done((bf16[4,128,1024]{1,2,0:T(8,128)(2,1)S(1)}, bf16[4,128,1024]{1,2,0:T(8,128)(2,1)S(1)}, u32[]{:S(2)}, u32[]{:S(2)}) %collective-permute-start) | collective-permute-done | bytes 1048608 | tf_op jit(solution)/shard_map/ppermute | solution.py:17
  53.5 4.2 %collective-permute-done.1 = bf16[4,128,1024]{1,2,0:T(8,128)(2,1)S(1)} collective-permute-done((bf16[4,128,1024]{1,2,0:T(8,128)(2,1)S(1)}, bf16[4,128,1024]{1,2,0:T(8,128)(2,1)S(1)}, u32[]{:S(2)}, u32[]{:S(2)}) %collective-permute-start.1) | collective-permute-done | bytes 1048608 | tf_op jit(solution)/shard_map/ppermute | solution.py:18
  57.7 0.4 pad_maximum_fusion
  58.1 2.9 %copy.16 = bf16[12,128,1024]{2,1,0:T(8,128)(2,1)} copy(bf16[12,128,1024]{1,2,0:T(8,128)(2,1)S(1)} %pad_maximum_fusion) | data formatting | bytes 6291456 | tf_op jit(solution)/shard_map/concatenate | solution.py:19
  61.0 0.0 all-gather.3.cloned.1.call-update
  61.0 0.6 copy-done.2
  61.7 0.7 fusion.35
  72.2 0.7 fusion.31
  72.9 0.1 compare_reduce_fusion
  73.0 0.0 copy-done.3
  73.0 0.3 fusion.28
  73.3 0.7 fusion.34
  73.9 3.0 %all-gather.3.cloned.1.call-done = bf16[24,128,1024]{2,1,0:T(8,128)(2,1)} async-done(((bf16[12,128,1024]{2,1,0:T(8,128)(2,1)}), bf16[24,128,1024]{2,1,0:T(8,128)(2,1)}) %all-gather.3.cloned.1.call-update) | async-done | bytes 6291472 | tf_op jit(solution)/shard_map/all_gather | solution.py:43
  76.9 19.0 %fusion.1 = bf16[1,1,4,128,1024]{4,3,2,1,0:T(8,128)(2,1)} fusion(bf16[2,12,128,1024]{3,2,1,0:T(8,128)(2,1)} %bitcast.70, s32[]{:T(128)S(6)} %add.344, s32[]{:T(128)S(6)} %select_n.52, s32[]{:T(128)S(6)} %select_n.51, s32[]{:T(128)S(6)} %select_n.50, s32[]{:T(128)S(6)} %select_n.49, s32[]{:T(128)S(6)} %select_n.48, s32[]{:T(128)S(6)} %select_n.47, ...), kind=kLoop, calls=%fused_computation.3 | loop fusion | flops 25690112 | bytes 17829988 | tf_op jit(solution)/shard_map/convert_element_type | solution.py:60
  (8 shorter events, 0.0 us)
Async XLA Ops:
  6.5 66.5 %copy-start = (f32[4,8]{1,0:T(4,128)S(1)}, f32[4,8]{1,0:T(4,128)}, u32[]{:S(2)}) copy-start(f32[4,8]{1,0:T(4,128)} %param.10) | copy-start | bytes 388
  6.5 1.6 %copy-start.1 = (bf16[1,1,1,512,1024]{4,3,2,1,0:T(8,128)(2,1)S(1)}, bf16[1,1,1,512,1024]{4,3,2,1,0:T(8,128)(2,1)}, u32[]{:S(2)}) copy-start(bf16[1,1,1,512,1024]{4,3,2,1,0:T(8,128)(2,1)} %param.6) | copy-start | bytes 3145732
  6.5 70.4 %all-gather.3.cloned.1.call-start = ((), (), s32[]{:S(2)}) async-start(), calls=%async_computation.1 | async-start | bytes 9437184 | tf_op jit(solution)/shard_map/all_gather | solution.py:43
  29.1 24.4 %collective-permute-start = (bf16[4,128,1024]{1,2,0:T(8,128)(2,1)S(1)}, bf16[4,128,1024]{1,2,0:T(8,128)(2,1)S(1)}, u32[]{:S(2)}, u32[]{:S(2)}) collective-permute-start(bf16[4,128,1024]{1,2,0:T(8,128)(2,1)S(1)} %bitcast.71), channel_id=1, source_target_pairs={{0,1},{1,2},{2,3},{4,5},{5,6},{6,7},{8,9},{9,10},{10,11},{12,13},{... | collective-permute-start | bytes 3145736 | tf_op jit(solution)/shard_map/ppermute | solution.py:17
  32.7 25.0 %collective-permute-start.1 = (bf16[4,128,1024]{1,2,0:T(8,128)(2,1)S(1)}, bf16[4,128,1024]{1,2,0:T(8,128)(2,1)S(1)}, u32[]{:S(2)}, u32[]{:S(2)}) collective-permute-start(bf16[4,128,1024]{1,2,0:T(8,128)(2,1)S(1)} %bitcast.72), channel_id=1, source_target_pairs={{1,0},{2,1},{3,2},{5,4},{6,5},{7,6},{9,8},{10,9},{11,10},{13,12},{... | collective-permute-start | bytes 3145736 | tf_op jit(solution)/shard_map/ppermute | solution.py:18
  61.0 0.7 copy-start.2
  61.0 12.0 %copy-start.3 = (s32[4]{0:T(128)S(1)}, s32[4]{0:T(128)}, u32[]{:S(2)}) copy-start(s32[4]{0:T(128)} %param.8) | copy-start | bytes 52
Sparse Core Ops, SparseCore 0:
  61.2 15.7 all-gather.2
